TPU v7x, 32 devices: a whole 2x2x4 slice. The times are simulated.
32 devices in a mesh: ctx: 8 (over y, x, core), tp: 4 (over z).
Axes of the slice: x: 2, y: 2, z: 4, core: 2. Of those that a mesh axis runs over, the one named last changes fastest.
Arguments:
- tokens: bfloat16 [4096, 2048], P(('ctx', 'tp')), may hold values from -8 to 8
- projection: bfloat16 [2048, 640], P(None, 'tp'), may hold values from -0.125 to 0.125
- conv_weight: float32 [4, 640], P(None, 'tp'), may hold values from -2.5 to 2.5
Outputs:
- attended: bfloat16 [4096, 512], P('ctx', 'tp')
All inputs are finite; a program needn't handle non-finite values.
Results may differ from a plain program's by a relative error of at most 0.0032.
The roundings to bfloat16 on the way count: a program that leaves them out, or rounds other values in their place, can miss the bound.
Values may be sent and summed in bfloat16 or wider, within the bound.
No kernel may reach another device: no remote copies, remote signals or barrier semaphores. Data moves between devices by JAX's collectives and lax.ppermute only.
A program may use at most 64 MiB of HBM per device.

v0:
```python
import math
import jax
import jax.numpy as jnp
from jax import lax
from jax.sharding import PartitionSpec as P

FEAT = 16


def passed_along(shard, axis, by):
    length = lax.axis_size(axis)
    pairs = [(i, i + by) for i in range(length) if 0 <= i + by < length]
    return lax.ppermute(shard, axis, pairs)


def taylor(raw_vals):
    num_rows, width_feat = raw_vals.shape
    linear = raw_vals * width_feat ** (-0.25)
    quadratic = (raw_vals[:, :, None] * raw_vals[:, None, :]).reshape(
        num_rows, width_feat * width_feat
    )
    quadratic = quadratic * (1.0 / (math.sqrt(2.0) * math.sqrt(width_feat)))
    ones_col = jnp.ones((num_rows, 1), jnp.float32)
    return jnp.concatenate([ones_col, linear, quadratic], axis=1).astype(jnp.bfloat16)


def per_device(tokens, projection, conv_weight):
    kernel_len = conv_weight.shape[0]
    conv_lag = kernel_len - 1
    row_width = projection.shape[1]
    highest = lax.Precision.HIGHEST
    projected = jnp.dot(
        lax.all_gather(tokens, "tp", axis=0, tiled=True),
        projection,
        preferred_element_type=jnp.float32,
    ).astype(jnp.bfloat16)
    rim_rows = passed_along(projected[projected.shape[0] - conv_lag :], "ctx", 1)
    local_rows = projected.shape[0]
    padded = jnp.concatenate([rim_rows, projected], axis=0).astype(jnp.float32)
    convolved = jnp.zeros((local_rows, row_width), jnp.float32)
    for offset in range(kernel_len):
        convolved = (
            convolved
            + conv_weight[offset] * padded[conv_lag - offset : conv_lag - offset + local_rows]
        )
    feat_query = taylor(convolved[:, :FEAT])
    feat_key = taylor(convolved[:, FEAT : 2 * FEAT])
    values = convolved[:, 2 * FEAT :].astype(jnp.bfloat16)
    num_feat = feat_key.shape[1]
    val_width = values.shape[1]
    local_state = jnp.einsum("tp,tv->pv", feat_key, values, preferred_element_type=jnp.float32)
    local_total = jnp.sum(feat_key.astype(jnp.float32), axis=0)
    empty_state = jnp.zeros((num_feat, val_width), jnp.float32)
    empty_total = jnp.zeros((num_feat,), jnp.float32)
    position = lax.axis_index("ctx")
    states = lax.all_gather(local_state[None], "ctx", axis=0, tiled=True)
    sums = lax.all_gather(local_total[None], "ctx", axis=0, tiled=True)
    earlier_mask = jnp.arange(states.shape[0]) < position
    new_state = jnp.sum(jnp.where(earlier_mask[:, None, None], states, 0.0), axis=0)
    new_total = jnp.sum(jnp.where(earlier_mask[:, None], sums, 0.0), axis=0)
    block_rows = min(local_rows, 768)
    num_blocks = local_rows // block_rows
    query_blocks = feat_query.reshape(num_blocks, block_rows, num_feat)
    key_blocks = feat_key.reshape(num_blocks, block_rows, num_feat)
    value_blocks = values.reshape(num_blocks, block_rows, val_width)
    causal = jnp.arange(block_rows)[:, None] >= jnp.arange(block_rows)[None, :]

    def block_step(carried, blocks):
        run_state, run_total = carried
        query_blk, key_blk, value_blk = blocks
        scores = jnp.einsum("ip,jp->ij", query_blk, key_blk, preferred_element_type=jnp.float32)
        scores = jnp.where(causal, scores, 0.0)
        numerator = jnp.dot(
            scores.astype(jnp.bfloat16), value_blk, preferred_element_type=jnp.float32
        )
        denominator = jnp.sum(scores, axis=1)
        query_wide = query_blk.astype(jnp.float32)
        numerator = numerator + jnp.dot(query_wide, run_state, precision=highest)
        denominator = denominator + jnp.dot(query_wide, run_total, precision=highest)
        run_state = run_state + jnp.einsum(
            "tp,tv->pv", key_blk, value_blk, preferred_element_type=jnp.float32
        )
        run_total = run_total + jnp.sum(key_blk.astype(jnp.float32), axis=0)
        return ((run_state, run_total), (numerator, denominator))

    _, (numerator, denominator) = lax.scan(
        block_step, (empty_state, empty_total), (query_blocks, key_blocks, value_blocks)
    )
    numerator = numerator.reshape(local_rows, val_width)
    denominator = denominator.reshape(local_rows)
    query_wide = feat_query.astype(jnp.float32)
    numerator = numerator + jnp.dot(query_wide, new_state, precision=highest)
    denominator = denominator + jnp.dot(query_wide, new_total, precision=highest)
    return (numerator / denominator[:, None]).astype(jnp.bfloat16)


def solution(mesh):
    return jax.shard_map(
        per_device,
        mesh=mesh,
        in_specs=(P(("ctx", "tp"), None), P(None, "tp"), P(None, "tp")),
        out_specs=P("ctx", "tp"),
        check_vma=False,
    )
```

profile of v0, /device:TPU:0, one launch (start us, length us, event | category | flops | bytes accessed | tf_op | source)
XLA Modules:
  0.0 101.6 jit_solution(15885712231923730799)
XLA Ops:
  6.5 0.7 all-gather.6.cloned.1.call-update
  7.3 0.0 all-gather.8.cloned.1.call-start
  7.3 0.8 fusion.12
  8.2 49.2 %all-gather.6.cloned.1.call-done = bf16[512,2048]{1,0:T(8,128)(2,1)} async-done(((bf16[128,2048]{1,0:T(8,128)(2,1)}), bf16[512,2048]{1,0:T(8,128)(2,1)}) %all-gather.6.cloned.1.call-update) | async-done | bytes 2097168 | tf_op jit(solution)/shard_map/all_gather | solution.py:33
  57.3 2.4 %convolution_convert_fusion = bf16[512,160]{0,1:T(8,128)(2,1)S(1)} fusion(bf16[512,2048]{1,0:T(8,128)(2,1)} %all-gather.6.cloned.1.call-done, bf16[2048,160]{0,1:T(8,128)(2,1)S(1)} %copy-done), kind=kOutput, calls=%fused_computation.4 | convolution fusion | flops 335626240 | bytes 2916352 | tf_op jit(solution)/shard_map/dot_general | solution.py:32
  59.8 0.1 slice.49
  59.8 1.6 %collective-permute-start = (bf16[3,160]{0,1:T(8,128)(2,1)S(1)}, bf16[3,160]{0,1:T(8,128)(2,1)S(1)}, u32[]{:S(2)}, u32[]{:S(2)}) collective-permute-start(bf16[3,160]{0,1:T(8,128)(2,1)S(1)} %slice.49), channel_id=1, source_target_pairs={{0,4},{4,8},{8,12},{12,16},{16,20},{20,24},{24,28},{1,5},{5,9},{9,... | collective-permute-start | bytes 2888 | tf_op jit(solution)/shard_map/ppermute | solution.py:13
  61.5 0.6 dynamic-slice.3
  62.7 0.1 maximum_convert_fusion
  62.8 0.4 fusion.4
  63.3 0.9 convolution_bitcast_fusion
  64.3 0.2 convert_reduce_fusion
  64.6 0.3 dynamic-update-slice
  64.8 24.9 %all-reduce = f32[2184]{0:T(1024)S(1)} all-reduce(f32[2184]{0:T(1024)S(1)} %dynamic-update-slice), channel_id=3, replica_groups=mesh['ctx'=8,'tp'=4] {'ctx'}, use_global_device_ids=true, to_apply=%add | all-reduce | flops 2184 | bytes 17472
  89.7 0.1 reshape.41
  89.8 0.1 select_reduce_fusion.1
  89.9 0.1 pad_maximum_fusion
  90.1 0.2 fusion.8
  90.3 0.2 fusion.14
  90.5 0.6 fusion.13
  91.1 0.3 fusion.2
  91.5 0.6 convolution_add_fusion.1
  92.1 1.4 %select_reduce_fusion = f32[273,128]{1,0:T(8,128)S(1)} fusion(f32[8,273,128]{2,1,0:T(8,128)} %all-gather.8.cloned.1.call-done, pred[8]{0:T(512)(128)(4,1)S(1)} %iota_compare_fusion.1), kind=kLoop, calls=%fused_computation.6 | loop fusion | flops 524160 | bytes 1257992 | tf_op jit(solution)/shard_map/reduce_sum | solution.py:59
  93.5 1.3 %fusion.1 = bf16[512,128]{1,0:T(8,128)(2,1)} fusion(f32[512,128]{1,0:T(8,128)S(1)} %convolution_add_fusion.1, bf16[512,273]{0,1:T(8,128)(2,1)S(1)} %pad_maximum_fusion, f32[273,128]{1,0:T(8,128)S(1)} %select_reduce_fusion, f32[512]{0:T(512)S(1)} %add_add_fusion), kind=kOutput, calls=%fused_computation.5 | convolution fusion | flops 214892544 | bytes 814592 | tf_op jit(solution)/shard_map/dot_general | solution.py:92
  (16 shorter events, 0.2 us)
Async XLA Ops:
  6.5 50.8 %copy-start = (bf16[2048,160]{0,1:T(8,128)(2,1)S(1)}, bf16[2048,160]{0,1:T(8,128)(2,1)}, u32[]{:S(2)}) copy-start(bf16[2048,160]{0,1:T(8,128)(2,1)} %param.4) | copy-start | bytes 1966084
  6.5 50.8 %all-gather.6.cloned.1.call-start = ((), (), s32[]{:S(2)}) async-start(), calls=%async_computation | async-start | bytes 2621440 | tf_op jit(solution)/shard_map/all_gather | solution.py:33
  7.3 84.8 %all-gather.8.cloned.1.call-start = ((), (), s32[]{:S(2)}) async-start(), calls=%async_computation.1 | async-start | bytes 1290240 | tf_op jit(solution)/shard_map/all_gather | solution.py:56
  8.2 53.3 %copy-start.1 = (u32[32]{0:T(128)S(1)}, u32[32]{0:T(128)}, u32[]{:S(2)}) copy-start(u32[32]{0:T(128)} %constant.37) | copy-start | bytes 388
  59.8 2.9 %collective-permute-start = (bf16[3,160]{0,1:T(8,128)(2,1)S(1)}, bf16[3,160]{0,1:T(8,128)(2,1)S(1)}, u32[]{:S(2)}, u32[]{:S(2)}) collective-permute-start(bf16[3,160]{0,1:T(8,128)(2,1)S(1)} %slice.49), channel_id=1, source_target_pairs={{0,4},{4,8},{8,12},{12,16},{16,20},{20,24},{24,28},{1,5},{5,9},{9,... | collective-permute-start | bytes 2888 | tf_op jit(solution)/shard_map/ppermute | solution.py:13
Sparse Core Ops, SparseCore 0:
  8.9 48.3 all-gather.5
  64.7 25.1 all-gather.7
where the time goes:
time: 102 us
  waiting for transfers between devices  49.9 us (49%)
  blocking collectives  24.9 us (24%)
  between operations  14.2 us (14%)
  matrix products  6.61 us (6%)
  other arithmetic  2.53 us (2%)
  local copies, waits for them, and re-layouts  1.89 us (2%)
  starting transfers between devices  1.61 us (2%)
    all_gather x1, waiting for transfers between devices, per_device(): lax.all_gather(tokens, 'tp', axis=0, tiled=True)  49.2 us
    unnamed x1, blocking collectives  24.9 us
    dot_general x1, matrix products, per_device(): jnp.dot(lax.all_gather(tokens, 'tp', axis=0, tiled=True), projection, pre...  2.43 us
  transfers between devices with their start and end apart: 3, of which 1 were waited for; matrix products, arithmetic and copies ran while one was open for 4% of the time, Pallas kernels for 0%

commit v1 on v0

--- a/solution.py
+++ b/solution.py
@@ -5,6 +5,23 @@
 from jax.sharding import PartitionSpec as P
 
 FEAT = 16
+
+
+def in_order(blocks, dim):
+    blocks = jnp.moveaxis(blocks, 0, dim)
+    shape = blocks.shape
+    return blocks.reshape(*shape[:dim], shape[dim] * shape[dim + 1], *shape[dim + 2 :])
+
+
+def collect(shard, axis, dim):
+    size = lax.axis_size(axis)
+    right = [(i, (i + 1) % size) for i in range(size)]
+    blocks = [shard]
+    while len(blocks) < size:
+        blocks.append(lax.ppermute(blocks[-1], axis, right))
+    here = lax.axis_index(axis)
+    blocks = jnp.stack(blocks)[(here - jnp.arange(size)) % size]
+    return in_order(blocks, dim)
 
 
 def passed_along(shard, axis, by):
@@ -30,9 +47,7 @@
     row_width = projection.shape[1]
     highest = lax.Precision.HIGHEST
     projected = jnp.dot(
-        lax.all_gather(tokens, "tp", axis=0, tiled=True),
-        projection,
-        preferred_element_type=jnp.float32,
+        collect(tokens, "tp", 0), projection, preferred_element_type=jnp.float32
     ).astype(jnp.bfloat16)
     rim_rows = passed_along(projected[projected.shape[0] - conv_lag :], "ctx", 1)
     local_rows = projected.shape[0]

time: 102 us -> 121 us (1.19)
  waiting for transfers between devices: 49.9 us -> 62.3 us
  local copies, waits for them, and re-layouts: 1.89 us -> 4.67 us
  starting transfers between devices: 1.61 us -> 4.35 us
  other arithmetic: 2.53 us -> 4.16 us
    all_gather x1 -> x0, waiting for transfers between devices: 49.2 us -> none  [per_device(): lax.all_gather(tokens, 'tp', axis=0, tiled=True)]
    ppermute x0 -> x3, waiting for transfers between devices: none -> 42.1 us  [collect(): blocks.append(lax.ppermute(blocks[-1], axis, right))]
    all_gather x1, waiting for transfers between devices: 0.02 us -> 20.1 us  [per_device(): states = lax.all_gather(local_state[None], 'ctx', axis=0, tiled=True)]
    ppermute x0 -> x3, starting transfers between devices: none -> 3.06 us  [collect(): blocks.append(lax.ppermute(blocks[-1], axis, right))]
    gather x0 -> x1, local copies, waits for them, and re-layouts: none -> 2.03 us  [collect(): blocks = jnp.stack(blocks)[(here - jnp.arange(size)) % size]]
    another operation x3 -> x4, other arithmetic: 0.11 us -> 1.73 us  [the longest x1 1.62 us: collect(): blocks = jnp.stack(blocks)[(here - jnp.arange(size)) % size]]
  transfers between devices with their start and end apart: 3 -> 5, of which waited for: 1 -> 4; matrix products, arithmetic and copies ran while one was open for 4% -> 3% of each run, Pallas kernels for 0% -> 0%
where the time goes in v1:
time: 121 us
  waiting for transfers between devices  62.3 us (51%)
  blocking collectives  24.4 us (20%)
  between operations  14.2 us (12%)
  matrix products  6.63 us (5%)
  local copies, waits for them, and re-layouts  4.67 us (4%)
  starting transfers between devices  4.35 us (4%)
  other arithmetic  4.16 us (3%)
    ppermute x3, waiting for transfers between devices, collect(): blocks.append(lax.ppermute(blocks[-1], axis, right))  42.1 us
    unnamed x1, blocking collectives  24.4 us
    all_gather x1, waiting for transfers between devices, per_device(): states = lax.all_gather(local_state[None], 'ctx', axis=0, tiled=True)  20.1 us
    ppermute x3, starting transfers between devices, collect(): blocks.append(lax.ppermute(blocks[-1], axis, right))  3.06 us
    dot_general x1, matrix products, per_device(): jnp.dot(collect(tokens, 'tp', 0), projection, preferred_element_type=jnp....  2.45 us
  transfers between devices with their start and end apart: 5, of which 4 were waited for; matrix products, arithmetic and copies ran while one was open for 3% of the time, Pallas kernels for 0%

profile of v1, /device:TPU:0, one launch (start us, length us, event | category | flops | bytes accessed | tf_op | source)
XLA Modules:
  0.0 120.6 jit_solution(1843827754493620923)
XLA Ops:
  6.5 3.1 %collective-permute-start = (bf16[128,2048]{1,0:T(8,128)(2,1)}, bf16[128,2048]{1,0:T(8,128)(2,1)S(1)}, u32[]{:S(2)}, u32[]{:S(2)}) collective-permute-start(bf16[128,2048]{1,0:T(8,128)(2,1)} %param.3), channel_id=1, source_target_pairs={{0,1},{1,2},{2,3},{3,0},{4,5},{5,6},{6,7},{7,4},{8,9},{9,10},{10,1... | collective-permute-start | bytes 1572872 | tf_op jit(solution)/shard_map/ppermute | solution.py:21
  9.6 14.2 %collective-permute-done = bf16[128,2048]{1,0:T(8,128)(2,1)S(1)} collective-permute-done((bf16[128,2048]{1,0:T(8,128)(2,1)}, bf16[128,2048]{1,0:T(8,128)(2,1)S(1)}, u32[]{:S(2)}, u32[]{:S(2)}) %collective-permute-start) | collective-permute-done | bytes 524320 | tf_op jit(solution)/shard_map/ppermute | solution.py:21
  23.8 14.9 %collective-permute-done.1 = bf16[128,2048]{1,0:T(8,128)(2,1)S(1)} collective-permute-done((bf16[128,2048]{1,0:T(8,128)(2,1)S(1)}, bf16[128,2048]{1,0:T(8,128)(2,1)S(1)}, u32[]{:S(2)}, u32[]{:S(2)}) %collective-permute-start.1) | collective-permute-done | bytes 524320 | tf_op jit(solution)/shard_map/ppermute | solution.py:21
  38.7 0.9 fusion.14
  39.6 13.1 %collective-permute-done.2 = bf16[128,2048]{1,0:T(8,128)(2,1)S(1)} collective-permute-done((bf16[128,2048]{1,0:T(8,128)(2,1)S(1)}, bf16[128,2048]{1,0:T(8,128)(2,1)S(1)}, u32[]{:S(2)}, u32[]{:S(2)}) %collective-permute-start.2) | collective-permute-done | bytes 524320 | tf_op jit(solution)/shard_map/ppermute | solution.py:21
  52.7 0.8 copy-done.2
  53.5 1.6 %pad_maximum_fusion = bf16[4,128,2048]{2,1,0:T(8,128)(2,1)S(1)} fusion(bf16[1,128,2048]{2,1,0:T(8,128)(2,1)} %bitcast.37, bf16[1,128,2048]{2,1,0:T(8,128)(2,1)} %bitcast.36, bf16[1,128,2048]{2,1,0:T(8,128)(2,1)S(1)} %bitcast.35, bf16[1,128,2048]{2,1,0:T(8,128)(2,1)} %bitcast.34), kind=kLoop, calls=%fused_computation.1 | loop fusion | flops 3145728 | bytes 4194304 | tf_op jit(solution)/shard_map/stack | solution.py:23
  55.1 2.0 %gather_fusion = bf16[4,128,2048]{2,1,0:T(8,128)(2,1)} fusion(bf16[4,128,2048]{2,1,0:T(8,128)(2,1)S(1)} %pad_maximum_fusion, s32[1024]{0:T(1024)S(1)} %pad_clamp_fusion), kind=kCustom, calls=%fused_computation | custom fusion | bytes 4194320 | tf_op jit(solution)/shard_map/gather | solution.py:23
  57.1 2.4 %convolution_convert_fusion = bf16[512,160]{0,1:T(8,128)(2,1)S(1)} fusion(bf16[512,2048]{1,0:T(8,128)(2,1)} %bitcast.29, bf16[2048,160]{0,1:T(8,128)(2,1)S(1)} %copy-done), kind=kOutput, calls=%fused_computation.6 | convolution fusion | flops 335626240 | bytes 2916352 | tf_op jit(solution)/shard_map/dot_general | solution.py:49
  59.6 1.3 %collective-permute-start.3 = (bf16[3,160]{0,1:T(8,128)(2,1)S(1)}, bf16[3,160]{0,1:T(8,128)(2,1)S(1)}, u32[]{:S(2)}, u32[]{:S(2)}) collective-permute-start(bf16[3,160]{0,1:T(8,128)(2,1)S(1)} %slice.51), channel_id=1, source_target_pairs={{0,4},{4,8},{8,12},{12,16},{16,20},{20,24},{24,28},{1,5},{5,9},{9,... | collective-permute-start | bytes 2888 | tf_op jit(solution)/shard_map/ppermute | solution.py:30
  61.0 0.6 dynamic-slice.3
  62.4 0.4 fusion.4
  62.9 0.2 convert_reduce_fusion
  63.1 1.0 convolution_bitcast_fusion
  64.1 0.2 dynamic-update-slice
  64.2 24.4 %all-reduce = f32[2184]{0:T(1024)S(1)} all-reduce(f32[2184]{0:T(1024)S(1)} %dynamic-update-slice), channel_id=3, replica_groups=mesh['ctx'=8,'tp'=4] {'ctx'}, use_global_device_ids=true, to_apply=%add | all-reduce | flops 2184 | bytes 17472
  89.0 0.2 fusion.8
  89.3 0.2 fusion.16
  89.5 0.6 fusion.15
  90.1 0.3 fusion.2
  90.4 0.6 convolution_add_fusion.1
  91.0 20.1 %all-gather.5.cloned.1.call-done = f32[8,273,128]{2,1,0:T(8,128)} async-done(((f32[1,273,128]{2,1,0:T(8,128)}), f32[8,273,128]{2,1,0:T(8,128)}) %all-gather.5.cloned.1.call-update) | async-done | bytes 1118224 | tf_op jit(solution)/shard_map/all_gather | solution.py:71
  111.1 1.4 %select_reduce_fusion = f32[273,128]{1,0:T(8,128)S(1)} fusion(f32[8,273,128]{2,1,0:T(8,128)} %all-gather.5.cloned.1.call-done, pred[8]{0:T(512)(128)(4,1)S(1)} %iota_compare_fusion.1), kind=kLoop, calls=%fused_computation.8 | loop fusion | flops 524160 | bytes 1257992 | tf_op jit(solution)/shard_map/reduce_sum | solution.py:74
  112.5 1.3 %fusion.1 = bf16[512,128]{1,0:T(8,128)(2,1)} fusion(f32[512,128]{1,0:T(8,128)S(1)} %convolution_add_fusion.1, bf16[512,273]{0,1:T(8,128)(2,1)S(1)} %pad_maximum_fusion.1, f32[273,128]{1,0:T(8,128)S(1)} %select_reduce_fusion, f32[512]{0:T(512)S(1)} %add_add_fusion), kind=kOutput, calls=%fused_computation.7 | convolution fusion | flops 214892544 | bytes 814592 | tf_op jit(solution)/shard_map/dot_general | solution.py:107
  (27 shorter events, 0.7 us)
Async XLA Ops:
  6.5 50.6 %copy-start = (bf16[2048,160]{0,1:T(8,128)(2,1)S(1)}, bf16[2048,160]{0,1:T(8,128)(2,1)}, u32[]{:S(2)}) copy-start(bf16[2048,160]{0,1:T(8,128)(2,1)} %param.4) | copy-start | bytes 1966084
  6.5 104.6 %all-gather.5.cloned.1.call-start = ((), (), s32[]{:S(2)}) async-start(), calls=%async_computation | async-start | bytes 1290240 | tf_op jit(solution)/shard_map/all_gather | solution.py:71
  6.5 17.2 %collective-permute-start = (bf16[128,2048]{1,0:T(8,128)(2,1)}, bf16[128,2048]{1,0:T(8,128)(2,1)S(1)}, u32[]{:S(2)}, u32[]{:S(2)}) collective-permute-start(bf16[128,2048]{1,0:T(8,128)(2,1)} %param.3), channel_id=1, source_target_pairs={{0,1},{1,2},{2,3},{3,0},{4,5},{5,6},{6,7},{7,4},{8,9},{9,10},{10,1... | collective-permute-start | bytes 1572872 | tf_op jit(solution)/shard_map/ppermute | solution.py:21
  23.7 14.9 %collective-permute-start.1 = (bf16[128,2048]{1,0:T(8,128)(2,1)S(1)}, bf16[128,2048]{1,0:T(8,128)(2,1)S(1)}, u32[]{:S(2)}, u32[]{:S(2)}) collective-permute-start(bf16[128,2048]{1,0:T(8,128)(2,1)S(1)} %collective-permute-done), channel_id=1, source_target_pairs={{0,1},{1,2},{2,3},{3,0},{4,5},{5,6},{6,7},{7,4},{8,9},{9,10},{10,1... | collective-permute-start | bytes 1572872 | tf_op jit(solution)/shard_map/ppermute | solution.py:21
  38.6 14.0 %copy-start.1 = (bf16[128,2048]{1,0:T(8,128)(2,1)}, bf16[128,2048]{1,0:T(8,128)(2,1)S(1)}, u32[]{:S(2)}) copy-start(bf16[128,2048]{1,0:T(8,128)(2,1)S(1)} %collective-permute-done.1) | copy-start | bytes 1572868
  38.6 14.0 %collective-permute-start.2 = (bf16[128,2048]{1,0:T(8,128)(2,1)S(1)}, bf16[128,2048]{1,0:T(8,128)(2,1)S(1)}, u32[]{:S(2)}, u32[]{:S(2)}) collective-permute-start(bf16[128,2048]{1,0:T(8,128)(2,1)S(1)} %collective-permute-done.1), channel_id=1, source_target_pairs={{0,1},{1,2},{2,3},{3,0},{4,5},{5,6},{6,7},{7,4},{8,9},{9,10},{10,1... | collective-permute-start | bytes 1572872 | tf_op jit(solution)/shard_map/ppermute | solution.py:21
  52.7 0.8 copy-start.2
  57.1 3.9 %copy-start.3 = (u32[32]{0:T(128)S(1)}, u32[32]{0:T(128)}, u32[]{:S(2)}) copy-start(u32[32]{0:T(128)} %constant.57) | copy-start | bytes 388
  59.6 2.6 %collective-permute-start.3 = (bf16[3,160]{0,1:T(8,128)(2,1)S(1)}, bf16[3,160]{0,1:T(8,128)(2,1)S(1)}, u32[]{:S(2)}, u32[]{:S(2)}) collective-permute-start(bf16[3,160]{0,1:T(8,128)(2,1)S(1)} %slice.51), channel_id=1, source_target_pairs={{0,4},{4,8},{8,12},{12,16},{16,20},{20,24},{24,28},{1,5},{5,9},{9,... | collective-permute-start | bytes 2888 | tf_op jit(solution)/shard_map/ppermute | solution.py:30
Sparse Core Ops, SparseCore 0:
  88.9 22.1 all-gather.4
